TPU v7x, 32 devices: a whole 2x2x4 slice. The times are simulated.
32 devices in a mesh: seq: 4 (over x, core), exp: 8 (over z, y).
Axes of the slice: x: 2, y: 2, z: 4, core: 2. Of those that a mesh axis runs over, the one named last changes fastest.
Arguments:
- residual_in: bfloat16 [4096, 2048], P(('seq', 'exp')), may hold values from -8 to 8
- ssm_input: bfloat16 [4096, 2048], P(('seq', 'exp')), may hold values from -6 to 6
- ssm_b: bfloat16 [4096, 128], P(('seq', 'exp')), may hold values from -6 to 6
- ssm_c: bfloat16 [4096, 128], P(('seq', 'exp')), may hold values from -0.5 to 0.5
- log_decay: float32 [4096, 32], P(('seq', 'exp')), may hold values from -2 to 0, as said below
- skip_gain: float32 [32], replicated, may hold values from 0.5 to 1.5
- out_proj: bfloat16 [2048, 2048], replicated, may hold values from -0.125 to 0.125
- norm_gain: float32 [2048], replicated, may hold values from 0.5 to 1.5
- router: bfloat16 [2048, 16], replicated, may hold values from -1 to 1
- assignment: int32 [4096, 1], P(('seq', 'exp')), may hold values from 0 to 15; in each aligned block of 128 rows (0 to 127, 128 to 255, ...) at most 16 rows name the same one
- expert_gate: bfloat16 [32, 2048, 704], P(('seq', 'exp')), may hold values from -0.125 to 0.125
- expert_up: bfloat16 [32, 2048, 704], P(('seq', 'exp')), may hold values from -0.125 to 0.125
- expert_down: bfloat16 [32, 704, 2048], P(('seq', 'exp')), may hold values from -0.15625 to 0.15625
Outputs:
- layer_out: bfloat16 [4096, 2048], P(('seq', 'exp'))
- route_weight: float32 [4096], P(('seq', 'exp'))
Inputs may be any that keep to these rules, and one draw needn't show every extreme that they name: `log_decay`: every entry is negative. `assignment`: on the rows of one device no expert is named more than 16 times; in every draw some expert is named exactly 16 times on some device.
All inputs are finite; a program needn't handle non-finite values.
Results may differ from a plain program's by a relative error of at most 0.009.
Values may be sent and summed in bfloat16 or wider, within the bound.
A program may use at most 576 MiB of HBM per device.

v0:
```python
import jax
import jax.numpy as jnp
from jax import lax
from jax.sharding import PartitionSpec as P

BLOCK = 128
SINK_ITERS = 8


def entering(x, axis, combine, identity):
    devices, here = (lax.axis_size(axis), lax.axis_index(axis))
    everything = jax.tree.map(lambda part: lax.all_gather(part, axis), x)
    start = jax.tree.map(
        lambda part, zero: jnp.broadcast_to(jnp.asarray(zero, part.dtype), part.shape), x, identity
    )

    def turn(k, before):
        reached = k < here
        new = combine(before, jax.tree.map(lambda part: part[k], everything))
        return jax.tree.map(lambda a, b: jnp.where(reached, a, b), new, before)

    return lax.fori_loop(0, devices, turn, start)


def widen(per_head, width):
    return jnp.repeat(per_head, width // per_head.shape[-1], axis=-1)


def block_terms(values, b_blocks, c_blocks, decay):
    block_count, length, head_count, head_size = values.shape
    cumulative = jnp.cumsum(decay, axis=1)
    weight = jnp.sqrt(-jnp.expm1(2.0 * decay))
    scores = jnp.einsum("ktn,ksn->kts", c_blocks, b_blocks, preferred_element_type=jnp.float32)
    leading = jnp.swapaxes(cumulative, 1, 2)
    distance = leading[:, :, :, None] - leading[:, :, None, :]
    causal = jnp.arange(length)[:, None] >= jnp.arange(length)[None, :]
    decay_mix = jnp.where(causal, jnp.exp(jnp.minimum(distance, 0.0)), 0.0) * (
        jnp.swapaxes(weight, 1, 2)[:, :, None, :] * scores[:, None, :, :]
    )
    decay_mix = decay_mix.astype(jnp.bfloat16)
    inner_part = jnp.einsum(
        "khts,kshp->kthp", decay_mix, values, preferred_element_type=jnp.float32
    )
    inner_part = inner_part.reshape(block_count, length, head_count * head_size)
    tail_weight = jnp.exp(cumulative[:, -1:, :] - cumulative) * weight
    row_width = head_count * head_size
    flat_values = values.reshape(block_count, length, row_width)
    tail_in = (flat_values.astype(jnp.float32) * widen(tail_weight, row_width)).astype(jnp.bfloat16)
    block_state = jnp.einsum("ksn,ksc->knc", b_blocks, tail_in, preferred_element_type=jnp.float32)
    return (inner_part, cumulative, block_state)


def combine_states(earlier, following):
    factor = widen(jnp.exp(following[0]), earlier[1].shape[1])
    return (earlier[0] + following[0], factor[None, :] * earlier[1] + following[1])


def local_step(entry, pieces):
    total, state = pieces
    return (widen(jnp.exp(total), entry.shape[1])[None, :] * entry + state, entry)


def balance(kernel, chosen_hot):
    column = jnp.ones((kernel.shape[1],), jnp.float32)
    for sweep in range(SINK_ITERS):
        row_scale = 1.0 / jnp.sum(kernel * column[None, :], axis=1)
        column = 1.0 / lax.psum(jnp.sum(kernel * row_scale[:, None], axis=0), ("seq", "exp"))
    weighted = kernel * column[None, :]
    return (
        kernel.shape[1]
        * jnp.sum(jnp.where(chosen_hot, weighted, 0.0), axis=1)
        / jnp.sum(weighted, axis=1)
    )


def feed_forward(arrived, gate_full, up_full, down_full):
    sources, slots, model_width = arrived.shape
    flat = arrived.reshape(sources * slots, model_width)
    gate_val = jnp.dot(flat, gate_full, preferred_element_type=jnp.float32)
    up_val = jnp.dot(flat, up_full, preferred_element_type=jnp.float32)
    hidden = (jax.nn.silu(gate_val) * up_val).astype(jnp.bfloat16)
    return jnp.dot(hidden, down_full, preferred_element_type=jnp.float32).reshape(
        sources, slots, model_width
    )


def per_device(
    residual_in,
    ssm_input,
    ssm_b,
    ssm_c,
    log_decay,
    skip_gain,
    out_proj,
    norm_gain,
    router,
    assignment,
    expert_gate,
    expert_up,
    expert_down,
):
    head_count = skip_gain.shape[0]
    length, row_width = ssm_input.shape
    head_size = row_width // head_count
    state_size = ssm_b.shape[1]
    model_width = residual_in.shape[1]
    block_count = length // BLOCK
    values = ssm_input.reshape(block_count, BLOCK, head_count, head_size)
    b_blocks = ssm_b.reshape(block_count, BLOCK, state_size)
    c_blocks = ssm_c.reshape(block_count, BLOCK, state_size)
    decay = log_decay.reshape(block_count, BLOCK, head_count)
    inner_part, cumulative, block_state = block_terms(values, b_blocks, c_blocks, decay)
    block_total = cumulative[:, -1, :]
    device_state, local_entry = lax.scan(
        local_step, jnp.zeros_like(block_state[0]), (block_total, block_state)
    )
    prefix_log = jnp.cumsum(block_total, axis=0) - block_total
    device_log = jnp.sum(block_total, axis=0)
    identity = (jnp.zeros((head_count,), jnp.float32), jnp.zeros_like(device_state))
    earlier_log, carried_in = entering(
        (device_log, device_state), ("seq", "exp"), combine_states, identity
    )
    entry = widen(jnp.exp(prefix_log), row_width)[:, None, :] * carried_in[None] + local_entry
    entry_rounded = entry.astype(jnp.bfloat16)
    carried = widen(jnp.exp(cumulative), row_width) * jnp.einsum(
        "ktn,knc->ktc", c_blocks, entry_rounded, preferred_element_type=jnp.float32
    )
    skip_wide = widen(skip_gain, row_width)
    flat_values = ssm_input.reshape(block_count, BLOCK, row_width).astype(jnp.float32)
    scan_out = (
        (inner_part + carried + skip_wide[None, None, :] * flat_values)
        .reshape(length, row_width)
        .astype(jnp.bfloat16)
    )
    mixed = residual_in.astype(jnp.float32) + jnp.dot(
        scan_out, out_proj, preferred_element_type=jnp.float32
    )
    scale = lax.rsqrt(jnp.mean(mixed * mixed, axis=1, keepdims=True) + 1e-05)
    normed = (mixed * scale * norm_gain[None, :]).astype(jnp.bfloat16)
    kernel = jnp.exp(jnp.dot(normed, router, preferred_element_type=jnp.float32))
    experts = router.shape[1]
    capacity = 2 * length // experts
    chosen = assignment[:, 0]
    chosen_hot = chosen[:, None] == jnp.arange(experts, dtype=jnp.int32)[None, :]
    route_weight = balance(kernel, chosen_hot)
    hot_int = chosen_hot.astype(jnp.int32)
    slot = jnp.sum(jnp.cumsum(hot_int, axis=0) * hot_int, axis=1) - 1
    position = chosen * capacity + slot
    packed = jnp.zeros((experts * capacity, model_width), jnp.bfloat16).at[position].set(normed)
    doubled = jnp.broadcast_to(
        packed.reshape(experts, 1, capacity, model_width), (experts, 2, capacity, model_width)
    )
    doubled = doubled.reshape(2 * experts, capacity, model_width)
    partial_value = feed_forward(
        lax.all_to_all(doubled, ("seq", "exp"), split_axis=0, concat_axis=0, tiled=True),
        expert_gate[0],
        expert_up[0],
        expert_down[0],
    )
    returned = lax.all_to_all(
        partial_value.astype(jnp.bfloat16), ("seq", "exp"), split_axis=0, concat_axis=0, tiled=True
    ).astype(partial_value.dtype)
    summed = jnp.sum(returned.reshape(experts, 2, capacity, model_width), axis=1).astype(
        jnp.bfloat16
    )
    summed = summed.reshape(experts * capacity, model_width)
    expert_out = summed[position]
    layer_out = (mixed + route_weight[:, None] * expert_out.astype(jnp.float32)).astype(
        jnp.bfloat16
    )
    return (layer_out, route_weight)


def solution(mesh):
    in_specs = (
        P(("seq", "exp"), None),
        P(("seq", "exp"), None),
        P(("seq", "exp"), None),
        P(("seq", "exp"), None),
        P(("seq", "exp"), None),
        P(),
        P(),
        P(),
        P(),
        P(("seq", "exp"), None),
        P(("seq", "exp"), None, None),
        P(("seq", "exp"), None, None),
        P(("seq", "exp"), None, None),
    )
    out_specs = (P(("seq", "exp"), None), P(("seq", "exp")))
    return jax.shard_map(
        per_device, mesh=mesh, in_specs=in_specs, out_specs=out_specs, check_vma=False
    )
```

profile of v0, /device:TPU:0, one launch (start us, length us, event | category | flops | bytes accessed | tf_op | source)
XLA Modules:
  0.0 762.2 jit_solution(15610699507661942850)
XLA Ops:
  19.5 69.7 %all-gather = f32[32,1,32]{2,1,0:T(1,128)S(1)} all-gather(f32[1,1,32]{2,1,0:T(1,128)} %get-tuple-element.165), channel_id=2, replica_groups=mesh['seq'=4,'exp'=8] {'seq','exp'}, dimensions={0}, use_global_device_ids=true | all-gather | bytes 4224 | tf_op jit(solution)/shard_map/all_gather | solution.py:12
  94.2 108.1 %all-gather.4.cloned.1.call-done = f32[4096,2048]{0,1:T(8,128)} async-done(((f32[128,2048]{0,1:T(8,128)}), f32[4096,2048]{0,1:T(8,128)}) %all-gather.4.cloned.1.call-update) | async-done | bytes 33554448 | tf_op jit(solution)/shard_map/all_gather | solution.py:12
  202.3 33.4 %copy.62 = f32[4096,2048]{1,0:T(8,128)} copy(f32[4096,2048]{0,1:T(8,128)} %all-gather.4.cloned.1.call-done) | data formatting | bytes 67108864
  235.7 92.5 %while.9 = (s32[]{:T(128)}, f32[128,2048]{1,0:T(8,128)}, s32[]{:T(128)}, f32[32,32]{1,0:T(8,128)S(1)}, f32[32,128,2048]{2,1,0:T(8,128)}, /*index=5*/s32[]{:T(128)}, s32[]{:T(128)}) while((s32[]{:T(128)}, f32[128,2048]{1,0:T(8,128)}, s32[]{:T(128)}, f32[32,32]{1,0:T(8,128)S(1)}, f32[32,128,2048]{2,1,0:T(8,128)}, ...), condition=%wide.region_2.3_spmd.clone, body=%wide.region_1.2_spmd.clone.sunk | while | flops 1048580 | bytes 3178985 | solution.py:22
  244.3 2.7 fusion.50
  253.0 2.7 fusion.50
  329.3 7.1 multiply_reduce_fusion
  336.4 3.2 scatter_custom_fusion
  339.7 2.8 broadcast_in_dim.94
  342.4 6.6 all-to-all-start
  350.8 67.1 %psum.56 = f32[16]{0:T(128)S(1)} all-reduce(f32[16]{0:T(128)S(1)} %multiply_reduce_fusion.15), channel_id=1, replica_groups=mesh['seq'=4,'exp'=8] {'seq','exp'}, use_global_device_ids=true, to_apply=%region_6.7 | all-reduce | flops 16 | bytes 128 | tf_op jit(solution)/shard_map/psum | solution.py:67
  418.2 38.7 %psum.57 = f32[16]{0:T(128)S(1)} all-reduce(f32[16]{0:T(128)S(1)} %multiply_reduce_fusion.13), channel_id=1, replica_groups=mesh['seq'=4,'exp'=8] {'seq','exp'}, use_global_device_ids=true, to_apply=%region_9.10 | all-reduce | flops 16 | bytes 128 | tf_op jit(solution)/shard_map/psum | solution.py:67
  457.0 4.3 fusion.4
  461.3 4.3 fusion.14
  467.9 4.2 convolution_convert_fusion
  472.1 6.0 all-to-all-start.1
  478.2 68.7 %psum.58 = f32[16]{0:T(128)S(1)} all-reduce(f32[16]{0:T(128)S(1)} %multiply_reduce_fusion.11), channel_id=1, replica_groups=mesh['seq'=4,'exp'=8] {'seq','exp'}, use_global_device_ids=true, to_apply=%region_12.13 | all-reduce | flops 16 | bytes 128 | tf_op jit(solution)/shard_map/psum | solution.py:67
  547.2 38.5 %psum.59 = f32[16]{0:T(128)S(1)} all-reduce(f32[16]{0:T(128)S(1)} %multiply_reduce_fusion.9), channel_id=1, replica_groups=mesh['seq'=4,'exp'=8] {'seq','exp'}, use_global_device_ids=true, to_apply=%region_15.16 | all-reduce | flops 16 | bytes 128 | tf_op jit(solution)/shard_map/psum | solution.py:67
  585.9 41.5 %psum.60 = f32[16]{0:T(128)S(1)} all-reduce(f32[16]{0:T(128)S(1)} %multiply_reduce_fusion.7), channel_id=1, replica_groups=mesh['seq'=4,'exp'=8] {'seq','exp'}, use_global_device_ids=true, to_apply=%region_18.19 | all-reduce | flops 16 | bytes 128 | tf_op jit(solution)/shard_map/psum | solution.py:67
  627.7 38.5 %psum.61 = f32[16]{0:T(128)S(1)} all-reduce(f32[16]{0:T(128)S(1)} %multiply_reduce_fusion.5), channel_id=1, replica_groups=mesh['seq'=4,'exp'=8] {'seq','exp'}, use_global_device_ids=true, to_apply=%region_21.22 | all-reduce | flops 16 | bytes 128 | tf_op jit(solution)/shard_map/psum | solution.py:67
  666.4 41.5 %psum.62 = f32[16]{0:T(128)S(1)} all-reduce(f32[16]{0:T(128)S(1)} %multiply_reduce_fusion.3), channel_id=1, replica_groups=mesh['seq'=4,'exp'=8] {'seq','exp'}, use_global_device_ids=true, to_apply=%region_24.25 | all-reduce | flops 16 | bytes 128 | tf_op jit(solution)/shard_map/psum | solution.py:67
  708.2 38.7 %psum.63 = f32[16]{0:T(128)S(1)} all-reduce(f32[16]{0:T(128)S(1)} %multiply_reduce_fusion.1), channel_id=1, replica_groups=mesh['seq'=4,'exp'=8] {'seq','exp'}, use_global_device_ids=true, to_apply=%region_27.28 | all-reduce | flops 16 | bytes 128 | tf_op jit(solution)/shard_map/psum | solution.py:67
  747.0 3.3 bitcast_reduce_fusion
  750.4 2.8 gather_fusion
  (215 shorter events, 113.1 us)
Async XLA Ops:
  7.2 460.7 %copy-start = (bf16[1,704,2048]{2,1,0:T(8,128)(2,1)S(1)}, bf16[1,704,2048]{2,1,0:T(8,128)(2,1)}, u32[]{:S(2)}) copy-start(bf16[1,704,2048]{2,1,0:T(8,128)(2,1)} %param.27) | copy-start | bytes 8650756
  7.2 5.9 copy-start.2
  7.2 195.2 %all-gather.4.cloned.1.call-start = ((), (), s32[]{:S(2)}) async-start(), calls=%async_computation.2 | async-start | bytes 34603008 | tf_op jit(solution)/shard_map/all_gather | solution.py:12
  235.7 93.6 %copy-start.1 = (bf16[128,128]{1,0:T(8,128)(2,1)S(1)}, bf16[128,128]{1,0:T(8,128)(2,1)}, u32[]{:S(2)}) copy-start(bf16[128,128]{1,0:T(8,128)(2,1)} %param.18) | copy-start | bytes 98308
  235.7 93.6 %copy-start.5 = (f32[2048]{0:T(1024)S(1)}, f32[2048]{0:T(1024)}, u32[]{:S(2)}) copy-start(f32[2048]{0:T(1024)} %broadcast_in_dim.48) | copy-start | bytes 24580
  235.7 93.6 %copy-start.6 = (f32[2048]{0:T(1024)S(1)}, f32[2048]{0:T(1024)}, u32[]{:S(2)}) copy-start(f32[2048]{0:T(1024)} %mul.305) | copy-start | bytes 24580
  329.3 7.1 copy-start.4
  342.4 6.7 copy-start.3
  342.4 114.5 %all-to-all-start = ((bf16[32,16,2048]{2,1,0:T(8,128)(2,1)}), bf16[32,16,2048]{2,1,0:T(8,128)(2,1)}, u32[]{:S(2)}, u32[]{:S(2)}) async-start(bf16[32,16,2048]{2,1,0:T(8,128)(2,1)} %bitcast.101), calls=%async_computation | async-start | bytes 4194304 | tf_op jit(solution)/shard_map/all_to_all | solution.py:155
  457.0 4.3 copy-start.9
  472.1 274.8 %copy-start.7 = (s32[128,1]{0,1:T(1,128)S(1)}, s32[128,1]{0,1:T(1,128)}, u32[]{:S(2)}) copy-start(s32[128,1]{0,1:T(1,128)} %param.24) | copy-start | bytes 1540
  472.1 274.9 %all-to-all-start.1 = ((bf16[32,16,2048]{2,1,0:T(8,128)(2,1)}), bf16[32,16,2048]{2,1,0:T(8,128)(2,1)}, u32[]{:S(2)}, u32[]{:S(2)}) async-start(bf16[32,16,2048]{2,1,0:T(8,128)(2,1)} %convolution_convert_fusion), calls=%async_computation.1 | async-start | bytes 4194304 | tf_op jit(solution)/shard_map/all_to_all | solution.py:160
  747.0 6.2 copy-start.8
Sparse Core Ops, SparseCore 0:
  15.2 187.0 all-gather.3
where the time goes:
time: 765 us; the launch traced here: 762 us
  blocking collectives  443 us (58%)
  waiting for transfers between devices  108 us (14%)
  other arithmetic  102 us (13%)
  local copies, waits for them, and re-layouts  54.4 us (7%)
  matrix products  27.2 us (4%)
  between operations  14.3 us (2%)
  starting transfers between devices  12.7 us (2%)
    psum x8, blocking collectives, balance(): lax.psum(jnp.sum(kernel * row_scale[:, None], axis=0), ('seq', 'exp'))  373 us
    all_gather x1, waiting for transfers between devices, entering(): everything = jax.tree.map(lambda part: lax.all_gather(part, axis), x)  108 us
    select_n x32, other arithmetic, turn(): return jax.tree.map(lambda a, b: jnp.where(reached, a, b), new, before)  87.5 us
    all_gather x1, blocking collectives, entering(): everything = jax.tree.map(lambda part: lax.all_gather(part, axis), x)  69.7 us
    unnamed x22, local copies, waits for them, and re-layouts  34.7 us
  transfers between devices with their start and end apart: 3, of which 1 were waited for; matrix products, arithmetic and copies ran while one was open for 2% of the time, Pallas kernels for 0%

commit v1 on v0

--- a/solution.py
+++ b/solution.py
@@ -2,6 +2,7 @@
 import jax.numpy as jnp
 from jax import lax
 from jax.sharding import PartitionSpec as P
+from jax.lax import psum
 
 BLOCK = 128
 SINK_ITERS = 8
@@ -64,7 +65,9 @@
     column = jnp.ones((kernel.shape[1],), jnp.float32)
     for sweep in range(SINK_ITERS):
         row_scale = 1.0 / jnp.sum(kernel * column[None, :], axis=1)
-        column = 1.0 / lax.psum(jnp.sum(kernel * row_scale[:, None], axis=0), ("seq", "exp"))
+        column = 1.0 / psum(
+            psum(jnp.sum(kernel * row_scale[:, None], axis=0), "exp"), axis_name="seq"
+        )
     weighted = kernel * column[None, :]
     return (
         kernel.shape[1]

time: 765 us -> 658 us (0.86)
  blocking collectives: 443 us -> 339 us
    psum x8 -> x16, blocking collectives: 373 us -> 269 us  [the longest x8 224 us: balance(): psum(jnp.sum(kernel * row_scale[:, None], axis=0), 'exp')]
where the time goes in v1:
time: 658 us; the launch traced here: 656 us
  blocking collectives  339 us (52%)
  waiting for transfers between devices  108 us (16%)
  other arithmetic  102 us (16%)
  local copies, waits for them, and re-layouts  54.4 us (8%)
  matrix products  27.2 us (4%)
  between operations  14.3 us (2%)
  starting transfers between devices  10.3 us (2%)
    psum x8, blocking collectives, balance(): psum(jnp.sum(kernel * row_scale[:, None], axis=0), 'exp')  224 us
    all_gather x1, waiting for transfers between devices, entering(): everything = jax.tree.map(lambda part: lax.all_gather(part, axis), x)  108 us
    select_n x32, other arithmetic, turn(): return jax.tree.map(lambda a, b: jnp.where(reached, a, b), new, before)  87.5 us
    all_gather x1, blocking collectives, entering(): everything = jax.tree.map(lambda part: lax.all_gather(part, axis), x)  69.7 us
    psum x8, blocking collectives, balance(): psum(psum(jnp.sum(kernel * row_scale[:, None], axis=0), 'exp'), axis_name...  45.4 us
    unnamed x22, local copies, waits for them, and re-layouts  34.7 us
  transfers between devices with their start and end apart: 3, of which 1 were waited for; matrix products, arithmetic and copies ran while one was open for 2% of the time, Pallas kernels for 0%

profile of v1, /device:TPU:0, one launch (start us, length us, event | category | flops | bytes accessed | tf_op | source)
XLA Modules:
  0.0 655.6 jit_solution(3492578408763274275)
XLA Ops:
  19.5 69.7 %all-gather = f32[32,1,32]{2,1,0:T(1,128)S(1)} all-gather(f32[1,1,32]{2,1,0:T(1,128)} %get-tuple-element.165), channel_id=2, replica_groups=mesh['seq'=4,'exp'=8] {'seq','exp'}, dimensions={0}, use_global_device_ids=true | all-gather | bytes 4224 | tf_op jit(solution)/shard_map/all_gather | solution.py:13
  94.2 108.1 %all-gather.4.cloned.1.call-done = f32[4096,2048]{0,1:T(8,128)} async-done(((f32[128,2048]{0,1:T(8,128)}), f32[4096,2048]{0,1:T(8,128)}) %all-gather.4.cloned.1.call-update) | async-done | bytes 33554448 | tf_op jit(solution)/shard_map/all_gather | solution.py:13
  202.3 33.4 %copy.62 = f32[4096,2048]{1,0:T(8,128)} copy(f32[4096,2048]{0,1:T(8,128)} %all-gather.4.cloned.1.call-done) | data formatting | bytes 67108864
  235.7 92.5 %while.9 = (s32[]{:T(128)}, f32[128,2048]{1,0:T(8,128)}, s32[]{:T(128)}, f32[32,32]{1,0:T(8,128)S(1)}, f32[32,128,2048]{2,1,0:T(8,128)}, /*index=5*/s32[]{:T(128)}, s32[]{:T(128)}) while((s32[]{:T(128)}, f32[128,2048]{1,0:T(8,128)}, s32[]{:T(128)}, f32[32,32]{1,0:T(8,128)S(1)}, f32[32,128,2048]{2,1,0:T(8,128)}, ...), condition=%wide.region_2.3_spmd.clone, body=%wide.region_1.2_spmd.clone.sunk | while | flops 1048580 | bytes 3178985 | solution.py:23
  329.3 7.1 %multiply_reduce_fusion = (f32[128]{0:T(128)S(1)}, f32[128,2048]{1,0:T(8,128)}) fusion(bf16[2048,2048]{1,0:T(8,128)(2,1)} %param.21, f32[128,2048]{0,1:T(8,128)} %bitcast.105, f32[128,2048]{0,1:T(8,128)} %bitcast.104, bf16[128,128]{1,0:T(8,128)(2,1)S(1)} %copy-done.1, bf16[128,2048]{0,1:T(8,128)(2,1)S(1)} %copy.55, f32[128,2048]{1,0:T(8,128)} %get-tuple-element.111, ...), kind=kOutput, calls=%fused_computation.30 | convolution fusion | flops 1143996288 | bytes 13681152 | tf_op jit(solution)/shard_map/dot_general | solution.py:138
  342.4 6.6 %all-to-all-start = ((bf16[32,16,2048]{2,1,0:T(8,128)(2,1)}), bf16[32,16,2048]{2,1,0:T(8,128)(2,1)}, u32[]{:S(2)}, u32[]{:S(2)}) async-start(bf16[32,16,2048]{2,1,0:T(8,128)(2,1)} %bitcast.101), calls=%async_computation | async-start | bytes 4194304 | tf_op jit(solution)/shard_map/all_to_all | solution.py:158
  350.8 48.6 %psum.112 = f32[16]{0:T(128)S(1)} all-reduce(f32[16]{0:T(128)S(1)} %multiply_reduce_fusion.15), channel_id=1, replica_groups=mesh['seq'=4,'exp'=8] {'exp'}, use_global_device_ids=true, to_apply=%region_6.7 | all-reduce | flops 16 | bytes 128 | tf_op jit(solution)/shard_map/psum | solution.py:69
  399.4 5.6 psum.113
  405.3 26.2 %psum.114 = f32[16]{0:T(128)S(1)} all-reduce(f32[16]{0:T(128)S(1)} %multiply_reduce_fusion.13), channel_id=1, replica_groups=mesh['seq'=4,'exp'=8] {'exp'}, use_global_device_ids=true, to_apply=%region_10.11 | all-reduce | flops 16 | bytes 128 | tf_op jit(solution)/shard_map/psum | solution.py:69
  431.5 5.6 psum.115
  437.3 4.3 fusion.4
  441.6 4.3 fusion.14
  456.1 49.8 %psum.116 = f32[16]{0:T(128)S(1)} all-reduce(f32[16]{0:T(128)S(1)} %multiply_reduce_fusion.11), channel_id=1, replica_groups=mesh['seq'=4,'exp'=8] {'exp'}, use_global_device_ids=true, to_apply=%region_14.15 | all-reduce | flops 16 | bytes 128 | tf_op jit(solution)/shard_map/psum | solution.py:69
  505.9 5.8 psum.117
  512.0 26.5 %psum.118 = f32[16]{0:T(128)S(1)} all-reduce(f32[16]{0:T(128)S(1)} %multiply_reduce_fusion.9), channel_id=1, replica_groups=mesh['seq'=4,'exp'=8] {'exp'}, use_global_device_ids=true, to_apply=%region_18.19 | all-reduce | flops 16 | bytes 128 | tf_op jit(solution)/shard_map/psum | solution.py:69
  538.4 5.6 psum.119
  544.3 17.2 %psum.120 = f32[16]{0:T(128)S(1)} all-reduce(f32[16]{0:T(128)S(1)} %multiply_reduce_fusion.7), channel_id=1, replica_groups=mesh['seq'=4,'exp'=8] {'exp'}, use_global_device_ids=true, to_apply=%region_22.23 | all-reduce | flops 16 | bytes 128 | tf_op jit(solution)/shard_map/psum | solution.py:69
  561.5 5.6 psum.121
  567.3 19.1 %psum.122 = f32[16]{0:T(128)S(1)} all-reduce(f32[16]{0:T(128)S(1)} %multiply_reduce_fusion.5), channel_id=1, replica_groups=mesh['seq'=4,'exp'=8] {'exp'}, use_global_device_ids=true, to_apply=%region_26.27 | all-reduce | flops 16 | bytes 128 | tf_op jit(solution)/shard_map/psum | solution.py:69
  586.5 5.6 psum.123
  592.4 17.1 %psum.124 = f32[16]{0:T(128)S(1)} all-reduce(f32[16]{0:T(128)S(1)} %multiply_reduce_fusion.3), channel_id=1, replica_groups=mesh['seq'=4,'exp'=8] {'exp'}, use_global_device_ids=true, to_apply=%region_30.31 | all-reduce | flops 16 | bytes 128 | tf_op jit(solution)/shard_map/psum | solution.py:69
  609.5 5.6 psum.125
  615.4 19.2 %psum.126 = f32[16]{0:T(128)S(1)} all-reduce(f32[16]{0:T(128)S(1)} %multiply_reduce_fusion.1), channel_id=1, replica_groups=mesh['seq'=4,'exp'=8] {'exp'}, use_global_device_ids=true, to_apply=%region_34.35 | all-reduce | flops 16 | bytes 128 | tf_op jit(solution)/shard_map/psum | solution.py:69
  634.6 5.6 psum.127
  (223 shorter events, 138.6 us)
Async XLA Ops:
  7.2 441.0 %copy-start = (bf16[1,704,2048]{2,1,0:T(8,128)(2,1)S(1)}, bf16[1,704,2048]{2,1,0:T(8,128)(2,1)}, u32[]{:S(2)}) copy-start(bf16[1,704,2048]{2,1,0:T(8,128)(2,1)} %param.27) | copy-start | bytes 8650756
  7.2 5.9 copy-start.2
  7.2 195.2 %all-gather.4.cloned.1.call-start = ((), (), s32[]{:S(2)}) async-start(), calls=%async_computation.2 | async-start | bytes 34603008 | tf_op jit(solution)/shard_map/all_gather | solution.py:13
  235.7 93.6 %copy-start.1 = (bf16[128,128]{1,0:T(8,128)(2,1)S(1)}, bf16[128,128]{1,0:T(8,128)(2,1)}, u32[]{:S(2)}) copy-start(bf16[128,128]{1,0:T(8,128)(2,1)} %param.18) | copy-start | bytes 98308
  235.7 93.6 %copy-start.5 = (f32[2048]{0:T(1024)S(1)}, f32[2048]{0:T(1024)}, u32[]{:S(2)}) copy-start(f32[2048]{0:T(1024)} %broadcast_in_dim.48) | copy-start | bytes 24580
  235.7 93.6 %copy-start.6 = (f32[2048]{0:T(1024)S(1)}, f32[2048]{0:T(1024)}, u32[]{:S(2)}) copy-start(f32[2048]{0:T(1024)} %mul.305) | copy-start | bytes 24580
  329.3 7.1 %copy-start.4 = (f32[2048]{0:T(1024)S(1)}, f32[2048]{0:T(1024)}, u32[]{:S(2)}) copy-start(f32[2048]{0:T(1024)} %param.22) | copy-start | bytes 24580
  342.4 6.7 %copy-start.3 = (bf16[2048,16]{0,1:T(8,128)(2,1)S(1)}, bf16[2048,16]{0,1:T(8,128)(2,1)}, u32[]{:S(2)}) copy-start(bf16[2048,16]{0,1:T(8,128)(2,1)} %param.23) | copy-start | bytes 196612
  342.4 94.8 %all-to-all-start = ((bf16[32,16,2048]{2,1,0:T(8,128)(2,1)}), bf16[32,16,2048]{2,1,0:T(8,128)(2,1)}, u32[]{:S(2)}, u32[]{:S(2)}) async-start(bf16[32,16,2048]{2,1,0:T(8,128)(2,1)} %bitcast.101), calls=%async_computation | async-start | bytes 4194304 | tf_op jit(solution)/shard_map/all_to_all | solution.py:158
  437.2 4.3 copy-start.9
  452.4 187.9 %copy-start.7 = (s32[128,1]{0,1:T(1,128)S(1)}, s32[128,1]{0,1:T(1,128)}, u32[]{:S(2)}) copy-start(s32[128,1]{0,1:T(1,128)} %param.24) | copy-start | bytes 1540
  452.4 188.0 %all-to-all-start.1 = ((bf16[32,16,2048]{2,1,0:T(8,128)(2,1)}), bf16[32,16,2048]{2,1,0:T(8,128)(2,1)}, u32[]{:S(2)}, u32[]{:S(2)}) async-start(bf16[32,16,2048]{2,1,0:T(8,128)(2,1)} %convolution_convert_fusion), calls=%async_computation.1 | async-start | bytes 4194304 | tf_op jit(solution)/shard_map/all_to_all | solution.py:163
  640.3 6.2 copy-start.8
Sparse Core Ops, SparseCore 0:
  15.2 187.0 all-gather.3
